TPU v7x, 128 devices: a whole 4x4x4 slice. The times are simulated.
128 devices in a mesh: dp: 16 (over z, y), mp: 8 (over x, core).
Axes of the slice: x: 4, y: 4, z: 4, core: 2. Of those that a mesh axis runs over, the one named last changes fastest.
Arguments:
- cotangent: bfloat16 [32768, 4096], P('dp'), may hold values from -64 to 64, as said below
- activation: bfloat16 [32768, 8192], P('dp', 'mp'), may hold values from -64 to 64, as said below
Outputs:
- update: bfloat16 [4096, 8192], P('dp', 'mp')
Inputs may be any that keep to these rules, and one draw needn't show every extreme that they name: `cotangent`: real-valued entries. `activation`: real-valued entries.
All inputs are finite; a program needn't handle non-finite values.
Results may differ from a plain program's by a relative error of at most 0.0054.
Values may be sent and summed in bfloat16 or wider, within the bound.
A program may use at most 256 MiB of HBM per device.

v0:
```python
import math
import jax
import jax.numpy as jnp
from jax import lax
from jax.sharding import PartitionSpec as P

N = 8192
ROWS = 4096
LINEAR_COEF = 3.4445
CUBIC_COEF = -4.775
QUINTIC_COEF = 2.0315
NORM_EPSILON = 1e-07
NORM_SHARE = 0.25
CONTRACT_FIRST = (((0,), (0,)), ((), ()))
CONTRACT_LAST = (((1,), (1,)), ((), ()))


def local(cotangent, activation):
    section = cotangent
    gradient = lax.psum_scatter(
        lax.dot_general(section, activation, CONTRACT_FIRST, preferred_element_type=jnp.float32),
        "dp",
        scatter_dimension=0,
        tiled=True,
    )
    sum_squares = lax.psum(jnp.sum(gradient * gradient), ("dp", "mp"))
    factor = NORM_SHARE * math.sqrt(ROWS) / (jnp.sqrt(sum_squares) + NORM_EPSILON)
    normalized = (gradient * factor).astype(jnp.bfloat16)
    weight_column = lax.all_gather(normalized, "dp", axis=0, tiled=True)
    section = weight_column
    gram_tile = lax.psum_scatter(
        lax.dot_general(section, normalized, CONTRACT_LAST, preferred_element_type=jnp.float32),
        "mp",
        scatter_dimension=0,
        tiled=True,
    ).T.astype(jnp.bfloat16)
    row_panel = lax.all_gather(gram_tile, "mp", axis=1, tiled=True)
    section = row_panel
    square_tile = jnp.dot(
        section,
        lax.all_gather(gram_tile, "dp", axis=0, tiled=True),
        preferred_element_type=jnp.float32,
    )
    polynomial = (CUBIC_COEF * gram_tile.astype(jnp.float32) + QUINTIC_COEF * square_tile).astype(
        jnp.bfloat16
    )
    section = weight_column
    product_tile = jnp.dot(
        lax.all_gather(polynomial, "mp", axis=1, tiled=True),
        section,
        preferred_element_type=jnp.float32,
    )
    rescale = math.sqrt(N)
    return (rescale * (LINEAR_COEF * normalized.astype(jnp.float32) + product_tile)).astype(
        jnp.bfloat16
    )


def solution(mesh):
    return jax.shard_map(
        local,
        mesh=mesh,
        in_specs=(P("dp", None), P("dp", "mp")),
        out_specs=P("dp", "mp"),
        check_vma=False,
    )
```

profile of v0, /device:TPU:1, one launch (start us, length us, event | category | flops | bytes accessed | tf_op | source)
XLA Modules:
  0.0 457.3 jit_solution(6413023268243869418)
XLA Ops:
  6.5 0.0 reduce-scatter.3.cloned.1.call-start
  6.5 23.7 %fusion.4 = f32[4096,1024]{1,0:T(8,128)} fusion(bf16[2048,4096]{1,0:T(8,128)(2,1)} %param.2, bf16[2048,1024]{1,0:T(8,128)(2,1)} %param.3), kind=kOutput, calls=%fused_computation.9 | convolution fusion | flops 17179869184 | bytes 37748736 | tf_op jit(solution)/shard_map/dot_general | solution.py:21
  30.3 0.0 reduce-scatter.3.cloned.1.call-update
  30.3 0.0 all-gather.5.cloned.1.call-start
  30.3 113.7 %reduce-scatter.3.cloned.1.call-done = f32[256,1024]{1,0:T(8,128)} async-done(((f32[4096,1024]{1,0:T(8,128)}), f32[256,1024]{1,0:T(8,128)}) %reduce-scatter.3.cloned.1.call-update) | async-done | bytes 1048592 | tf_op jit(solution)/shard_map/reduce_scatter | solution.py:20
  144.0 2.1 multiply_reduce_fusion
  146.1 64.8 %psum.7 = f32[]{:T(128)} all-reduce(f32[]{:T(128)} %multiply_reduce_fusion), channel_id=1, replica_groups=mesh['dp'=16,'mp'=8] {'dp','mp'}, use_global_device_ids=true, to_apply=%region_2.0 | all-reduce | flops 1 | bytes 8 | tf_op jit(solution)/shard_map/psum | solution.py:26
  211.6 2.1 multiply_convert_fusion
  213.7 0.0 all-gather.5.cloned.1.call-update
  213.7 0.0 reduce-scatter.5.cloned.1.call-start
  213.8 68.2 %all-gather.5.cloned.1.call-done = bf16[4096,1024]{1,0:T(8,128)(2,1)} async-done(((bf16[256,1024]{1,0:T(8,128)(2,1)}), bf16[4096,1024]{1,0:T(8,128)(2,1)}) %all-gather.5.cloned.1.call-update) | async-done | bytes 8388624 | tf_op jit(solution)/shard_map/all_gather | solution.py:29
  282.0 7.8 %fusion.5 = f32[4096,256]{1,0:T(8,128)} fusion(bf16[4096,1024]{1,0:T(8,128)(2,1)} %all-gather.5.cloned.1.call-done, bf16[256,1024]{1,0:T(8,128)(2,1)} %multiply_convert_fusion), kind=kOutput, calls=%fused_computation.10 | convolution fusion | flops 2147483648 | bytes 13107200 | tf_op jit(solution)/shard_map/dot_general | solution.py:32
  289.8 0.0 reduce-scatter.5.cloned.1.call-update
  289.8 0.0 all-gather.7.cloned.1.call-start
  289.9 34.7 %reduce-scatter.5.cloned.1.call-done = f32[512,256]{1,0:T(8,128)} async-done(((f32[4096,256]{1,0:T(8,128)}), f32[512,256]{1,0:T(8,128)}) %reduce-scatter.5.cloned.1.call-update) | async-done | bytes 524304 | tf_op jit(solution)/shard_map/reduce_scatter | solution.py:31
  324.5 1.8 convert_bitcast_fusion
  326.3 0.0 all-gather.7.cloned.1.call-update
  326.3 0.0 all-gather.9.cloned.1.call-start
  326.4 0.5 all-gather.9.cloned.1.call-update
  326.9 0.0 copy-start
  326.9 0.0 all-gather.11.cloned.1.call-start
  327.0 26.9 %all-gather.7.cloned.1.call-done = bf16[256,4096]{0,1:T(8,128)(2,1)} async-done(((bf16[256,512]{0,1:T(8,128)(2,1)}), bf16[256,4096]{0,1:T(8,128)(2,1)}) %all-gather.7.cloned.1.call-update) | async-done | bytes 2097168 | tf_op jit(solution)/shard_map/all_gather | solution.py:37
  353.9 58.8 %all-gather.9.cloned.1.call-done = bf16[4096,512]{0,1:T(8,128)(2,1)} async-done(((bf16[256,512]{0,1:T(8,128)(2,1)}), bf16[4096,512]{0,1:T(8,128)(2,1)}) %all-gather.9.cloned.1.call-update) | async-done | bytes 4194320 | tf_op jit(solution)/shard_map/all_gather | solution.py:41
  412.6 4.8 %fusion.3 = bf16[256,512]{0,1:T(8,128)(2,1)} fusion(bf16[4096,512]{0,1:T(8,128)(2,1)} %all-gather.9.cloned.1.call-done, bf16[256,4096]{0,1:T(8,128)(2,1)} %all-gather.7.cloned.1.call-done, bf16[256,512]{0,1:T(8,128)(2,1)} %convert_bitcast_fusion), kind=kOutput, calls=%fused_computation.5 | convolution fusion | flops 1074397184 | bytes 6815744 | tf_op jit(solution)/shard_map/dot_general | solution.py:39
  417.4 0.0 all-gather.11.cloned.1.call-update
  417.5 25.8 %all-gather.11.cloned.1.call-done = bf16[256,4096]{0,1:T(8,128)(2,1)} async-done(((bf16[256,512]{0,1:T(8,128)(2,1)}), bf16[256,4096]{0,1:T(8,128)(2,1)}) %all-gather.11.cloned.1.call-update) | async-done | bytes 2097168 | tf_op jit(solution)/shard_map/all_gather | solution.py:49
  443.3 0.0 copy-done
  443.3 7.2 %fusion.1 = bf16[256,1024]{1,0:T(8,128)(2,1)} fusion(bf16[256,4096]{0,1:T(8,128)(2,1)} %all-gather.11.cloned.1.call-done, bf16[4096,1024]{1,0:T(8,128)(2,1)} %all-gather.5.cloned.1.call-done, bf16[256,1024]{1,0:T(8,128)(2,1)S(1)} %copy-done), kind=kOutput, calls=%fused_computation.2 | convolution fusion | flops 2148794368 | bytes 11534336 | tf_op jit(solution)/shard_map/dot_general | solution.py:48
Async XLA Ops:
  6.5 137.5 %reduce-scatter.3.cloned.1.call-start = ((), (), s32[]{:S(2)}) async-start(), calls=%async_computation.2 | async-start | bytes 17825792 | tf_op jit(solution)/shard_map/reduce_scatter | solution.py:20
  30.3 251.7 %all-gather.5.cloned.1.call-start = ((), (), s32[]{:S(2)}) async-start(), calls=%async_computation.3 | async-start | bytes 8912896 | tf_op jit(solution)/shard_map/all_gather | solution.py:29
  213.7 110.8 %reduce-scatter.5.cloned.1.call-start = ((), (), s32[]{:S(2)}) async-start(), calls=%async_computation.4 | async-start | bytes 4718592 | tf_op jit(solution)/shard_map/reduce_scatter | solution.py:31
  289.8 64.1 %all-gather.7.cloned.1.call-start = ((), (), s32[]{:S(2)}) async-start(), calls=%async_computation.5 | async-start | bytes 2359296 | tf_op jit(solution)/shard_map/all_gather | solution.py:37
  326.3 86.3 %all-gather.9.cloned.1.call-start = ((), (), s32[]{:S(2)}) async-start(), calls=%async_computation.6 | async-start | bytes 4456448 | tf_op jit(solution)/shard_map/all_gather | solution.py:41
  326.9 116.3 %copy-start = (bf16[256,1024]{1,0:T(8,128)(2,1)S(1)}, bf16[256,1024]{1,0:T(8,128)(2,1)}, u32[]{:S(2)}) copy-start(bf16[256,1024]{1,0:T(8,128)(2,1)} %multiply_convert_fusion) | copy-start | bytes 1572868
  326.9 116.3 %all-gather.11.cloned.1.call-start = ((), (), s32[]{:S(2)}) async-start(), calls=%async_computation.7 | async-start | bytes 2359296 | tf_op jit(solution)/shard_map/all_gather | solution.py:49
Sparse Core Ops, SparseCore 0:
  30.4 113.5 reduce-scatter.2
  213.9 68.1 all-gather.4
  289.9 34.5 reduce-scatter.4
  326.5 27.3 all-gather.6
  355.8 56.7 all-gather.8
  417.6 25.6 all-gather.10
where the time goes:
time: 458 us; the launch traced here: 457 us
  waiting for transfers between devices  329 us (72%)
  blocking collectives  64.8 us (14%)
  matrix products  43.5 us (9%)
  between operations  14.2 us (3%)
  other arithmetic  6 us (1%)
    reduce_scatter x1, waiting for transfers between devices, local(): lax.psum_scatter(lax.dot_general(section, activation, CONTRACT_FIRST, pre...  114 us
    all_gather x1, waiting for transfers between devices, local(): weight_column = lax.all_gather(normalized, 'dp', axis=0, tiled=True)  68.2 us
    psum x1, blocking collectives, local(): sum_squares = lax.psum(jnp.sum(gradient * gradient), ('dp', 'mp'))  64.8 us
    all_gather x1, waiting for transfers between devices, local(): lax.all_gather(gram_tile, 'dp', axis=0, tiled=True)  58.8 us
    reduce_scatter x1, waiting for transfers between devices, local(): lax.psum_scatter(lax.dot_general(section, normalized, CONTRACT_LAST, pref...  34.7 us
    all_gather x1, waiting for transfers between devices, local(): row_panel = lax.all_gather(gram_tile, 'mp', axis=1, tiled=True)  26.9 us
    all_gather x1, waiting for transfers between devices, local(): lax.all_gather(polynomial, 'mp', axis=1, tiled=True)  25.8 us
    dot_general x1, matrix products, local(): lax.dot_general(section, activation, CONTRACT_FIRST, preferred_element_ty...  23.7 us
  transfers between devices with their start and end apart: 6, of which 6 were waited for; matrix products, arithmetic and copies ran while one was open for 0% of the time, Pallas kernels for 0%

commit v1 on v0

--- a/solution.py
+++ b/solution.py
@@ -1,8 +1,10 @@
+import functools
 import math
 import jax
 import jax.numpy as jnp
 from jax import lax
 from jax.sharding import PartitionSpec as P
+from jax.lax import axis_index, axis_size, ppermute
 
 N = 8192
 ROWS = 4096
@@ -13,6 +15,23 @@
 NORM_SHARE = 0.25
 CONTRACT_FIRST = (((0,), (0,)), ((), ()))
 CONTRACT_LAST = (((1,), (1,)), ((), ()))
+
+
+def define_halves_now(sheet, axis_tag, on_dim):
+    dev_count = axis_size(axis_tag)
+    found = []
+    for rr in [*range(dev_count)]:
+        found.append((rr, (rr + 1) % dev_count))
+    arr_next = [None] * dev_count
+    arr_next[dev_count - 1] = sheet
+    for u in range(dev_count - 2, -1, -1):
+        arr_next[u] = ppermute(arr_next[u + 1], perm=found, axis_name=axis_tag)
+    left_arr = jnp.concatenate(arr_next, axis=on_dim)
+    tile_out = (axis_index(axis_tag) + 1) * sheet.shape[on_dim]
+    return jnp.roll(left_arr, shift=tile_out, axis=on_dim)
+
+
+_touch_hubs = functools.partial(define_halves_now, axis_tag="mp", on_dim=1)
 
 
 def local(cotangent, activation):
@@ -34,7 +53,7 @@
         scatter_dimension=0,
         tiled=True,
     ).T.astype(jnp.bfloat16)
-    row_panel = lax.all_gather(gram_tile, "mp", axis=1, tiled=True)
+    row_panel = _touch_hubs(gram_tile)
     section = row_panel
     square_tile = jnp.dot(
         section,

time: 458 us -> 434 us (0.948)
  waiting for transfers between devices: 329 us -> 289 us
  local copies, waits for them, and re-layouts: 0.01 us -> 10.2 us
    all_gather x1, waiting for transfers between devices: 58.8 us -> 0.41 us  [local(): lax.all_gather(gram_tile, 'dp', axis=0, tiled=True)]
    ppermute x0 -> x7, waiting for transfers between devices: none -> 42.4 us  [define_halves_now(): arr_next[u] = ppermute(arr_next[u + 1], perm=found, axis_name=axis_tag)]
    all_gather x1 -> x0, waiting for transfers between devices: 26.9 us -> none  [local(): row_panel = lax.all_gather(gram_tile, 'mp', axis=1, tiled=True)]
    unnamed x2 -> x20, local copies, waits for them, and re-layouts: 0.01 us -> 10.2 us
  transfers between devices with their start and end apart: 6 -> 12, of which waited for: 6 -> 12; matrix products, arithmetic and copies ran while one was open for 0% -> 3% of each run, Pallas kernels for 0% -> 0%
where the time goes in v1:
time: 434 us; the launch traced here: 433 us
  waiting for transfers between devices  289 us (67%)
  blocking collectives  64.8 us (15%)
  matrix products  43.5 us (10%)
  between operations  13.9 us (3%)
  local copies, waits for them, and re-layouts  10.2 us (2%)
  other arithmetic  7.5 us (2%)
  starting transfers between devices  4.71 us (1%)
    reduce_scatter x1, waiting for transfers between devices, local(): lax.psum_scatter(lax.dot_general(section, activation, CONTRACT_FIRST, pre...  114 us
    all_gather x1, waiting for transfers between devices, local(): weight_column = lax.all_gather(normalized, 'dp', axis=0, tiled=True)  68.2 us
    psum x1, blocking collectives, local(): sum_squares = lax.psum(jnp.sum(gradient * gradient), ('dp', 'mp'))  64.8 us
    ppermute x7, waiting for transfers between devices, define_halves_now(): arr_next[u] = ppermute(arr_next[u + 1], perm=found, axis_name=axis_tag)  42.4 us
    reduce_scatter x1, waiting for transfers between devices, local(): lax.psum_scatter(lax.dot_general(section, normalized, CONTRACT_LAST, pref...  34.5 us
    all_gather x1, waiting for transfers between devices, local(): lax.all_gather(polynomial, 'mp', axis=1, tiled=True)  29.6 us
    dot_general x1, matrix products, local(): lax.dot_general(section, activation, CONTRACT_FIRST, preferred_element_ty...  23.7 us
    unnamed x20, local copies, waits for them, and re-layouts  10.2 us
  transfers between devices with their start and end apart: 12, of which 12 were waited for; matrix products, arithmetic and copies ran while one was open for 3% of the time, Pallas kernels for 0%

profile of v1, /device:TPU:1, one launch (start us, length us, event | category | flops | bytes accessed | tf_op | source)
XLA Modules:
  0.0 433.4 jit_solution(1217112252482850628)
XLA Ops:
  6.5 23.7 %fusion.14 = f32[4096,1024]{1,0:T(8,128)} fusion(bf16[2048,4096]{1,0:T(8,128)(2,1)} %param.2, bf16[2048,1024]{1,0:T(8,128)(2,1)} %param.3), kind=kOutput, calls=%fused_computation.28 | convolution fusion | flops 17179869184 | bytes 37748736 | tf_op jit(solution)/shard_map/dot_general | solution.py:40
  30.3 113.7 %reduce-scatter.3.cloned.1.call-done = f32[256,1024]{1,0:T(8,128)} async-done(((f32[4096,1024]{1,0:T(8,128)}), f32[256,1024]{1,0:T(8,128)}) %reduce-scatter.3.cloned.1.call-update) | async-done | bytes 1048592 | tf_op jit(solution)/shard_map/reduce_scatter | solution.py:39
  144.0 2.1 multiply_reduce_fusion
  146.1 64.8 %psum.7 = f32[]{:T(128)} all-reduce(f32[]{:T(128)} %multiply_reduce_fusion), channel_id=1, replica_groups=mesh['dp'=16,'mp'=8] {'dp','mp'}, use_global_device_ids=true, to_apply=%region_2.0 | all-reduce | flops 1 | bytes 8 | tf_op jit(solution)/shard_map/psum | solution.py:45
  211.6 2.1 multiply_convert_fusion
  213.8 68.2 %all-gather.4.cloned.1.call-done = bf16[4096,1024]{1,0:T(8,128)(2,1)} async-done(((bf16[256,1024]{1,0:T(8,128)(2,1)}), bf16[4096,1024]{1,0:T(8,128)(2,1)}) %all-gather.4.cloned.1.call-update) | async-done | bytes 8388624 | tf_op jit(solution)/shard_map/all_gather | solution.py:48
  282.0 7.8 %fusion.15 = f32[4096,256]{1,0:T(8,128)} fusion(bf16[4096,1024]{1,0:T(8,128)(2,1)} %all-gather.4.cloned.1.call-done, bf16[256,1024]{1,0:T(8,128)(2,1)} %multiply_convert_fusion), kind=kOutput, calls=%fused_computation.29 | convolution fusion | flops 2147483648 | bytes 13107200 | tf_op jit(solution)/shard_map/dot_general | solution.py:51
  289.9 34.5 %reduce-scatter.5.cloned.1.call-done = f32[512,256]{1,0:T(8,128)} async-done(((f32[4096,256]{1,0:T(8,128)}), f32[512,256]{1,0:T(8,128)}) %reduce-scatter.5.cloned.1.call-update) | async-done | bytes 524304 | tf_op jit(solution)/shard_map/reduce_scatter | solution.py:50
  324.4 1.8 convert_bitcast_fusion
  326.3 1.2 collective-permute-start
  327.5 3.7 collective-permute-done
  331.2 2.3 collective-permute-start.1
  333.5 4.7 %collective-permute-done.1 = bf16[256,512]{0,1:T(8,128)(2,1)S(1)} collective-permute-done((bf16[256,512]{0,1:T(8,128)(2,1)S(1)}, bf16[256,512]{0,1:T(8,128)(2,1)S(1)}, u32[]{:S(2)}, u32[]{:S(2)}) %collective-permute-start.1) | collective-permute-done | bytes 262176 | tf_op jit(solution)/shard_map/ppermute | solution.py:28
  338.2 1.1 collective-permute-start.2
  339.3 5.9 %collective-permute-done.2 = bf16[256,512]{0,1:T(8,128)(2,1)S(1)} collective-permute-done((bf16[256,512]{0,1:T(8,128)(2,1)S(1)}, bf16[256,512]{0,1:T(8,128)(2,1)S(1)}, u32[]{:S(2)}, u32[]{:S(2)}) %collective-permute-start.2) | collective-permute-done | bytes 262176 | tf_op jit(solution)/shard_map/ppermute | solution.py:28
  345.2 7.0 %collective-permute-done.3 = bf16[256,512]{0,1:T(8,128)(2,1)S(1)} collective-permute-done((bf16[256,512]{0,1:T(8,128)(2,1)S(1)}, bf16[256,512]{0,1:T(8,128)(2,1)S(1)}, u32[]{:S(2)}, u32[]{:S(2)}) %collective-permute-start.3) | collective-permute-done | bytes 262176 | tf_op jit(solution)/shard_map/ppermute | solution.py:28
  352.2 7.0 %collective-permute-done.4 = bf16[256,512]{0,1:T(8,128)(2,1)S(1)} collective-permute-done((bf16[256,512]{0,1:T(8,128)(2,1)S(1)}, bf16[256,512]{0,1:T(8,128)(2,1)S(1)}, u32[]{:S(2)}, u32[]{:S(2)}) %collective-permute-start.4) | collective-permute-done | bytes 262176 | tf_op jit(solution)/shard_map/ppermute | solution.py:28
  359.3 7.0 %collective-permute-done.5 = bf16[256,512]{0,1:T(8,128)(2,1)S(1)} collective-permute-done((bf16[256,512]{0,1:T(8,128)(2,1)S(1)}, bf16[256,512]{0,1:T(8,128)(2,1)S(1)}, u32[]{:S(2)}, u32[]{:S(2)}) %collective-permute-start.5) | collective-permute-done | bytes 262176 | tf_op jit(solution)/shard_map/ppermute | solution.py:28
  366.3 7.0 %collective-permute-done.6 = bf16[256,512]{0,1:T(8,128)(2,1)S(1)} collective-permute-done((bf16[256,512]{0,1:T(8,128)(2,1)S(1)}, bf16[256,512]{0,1:T(8,128)(2,1)S(1)}, u32[]{:S(2)}, u32[]{:S(2)}) %collective-permute-start.6) | collective-permute-done | bytes 262176 | tf_op jit(solution)/shard_map/ppermute | solution.py:28
  373.3 0.7 constant_dynamic-update-slice_fusion.15
  374.0 0.7 constant_dynamic-update-slice_fusion.14
  374.7 0.7 constant_dynamic-update-slice_fusion.13
  376.9 0.7 constant_dynamic-update-slice_fusion.10
  377.6 0.7 constant_dynamic-update-slice_fusion.9
  378.3 0.7 constant_dynamic-update-slice_fusion.8
  379.1 0.7 constant_dynamic-update-slice_fusion.7
  379.8 0.7 constant_dynamic-update-slice_fusion.6
  380.5 0.7 constant_dynamic-update-slice_fusion.5
  382.7 0.7 constant_dynamic-update-slice_fusion.2
  385.3 4.8 %fusion.10 = bf16[256,512]{0,1:T(8,128)(2,1)} fusion(bf16[4096,512]{0,1:T(8,128)(2,1)} %all-gather.6.cloned.1.call-done, bf16[256,8192]{0,1:T(8,128)(2,1)} %constant_dynamic-update-slice_fusion, s32[]{:T(128)S(6)} %select_n.14, bf16[256,512]{0,1:T(8,128)(2,1)S(1)} %copy-done.2), kind=kOutput, calls=%fused_computation.7 | convolution fusion | flops 1074397184 | bytes 6815748 | tf_op jit(solution)/shard_map/dot_general | solution.py:58
  390.1 29.6 %all-gather.8.cloned.1.call-done = bf16[256,4096]{0,1:T(8,128)(2,1)} async-done(((bf16[256,512]{0,1:T(8,128)(2,1)}), bf16[256,4096]{0,1:T(8,128)(2,1)}) %all-gather.8.cloned.1.call-update) | async-done | bytes 2097168 | tf_op jit(solution)/shard_map/all_gather | solution.py:68
  419.7 7.2 %fusion.3 = bf16[256,1024]{1,0:T(8,128)(2,1)} fusion(bf16[256,4096]{0,1:T(8,128)(2,1)} %all-gather.8.cloned.1.call-done, bf16[4096,1024]{1,0:T(8,128)(2,1)} %all-gather.4.cloned.1.call-done, bf16[256,1024]{1,0:T(8,128)(2,1)S(1)} %copy-done), kind=kOutput, calls=%fused_computation.4 | convolution fusion | flops 2148794368 | bytes 11534336 | tf_op jit(solution)/shard_map/dot_general | solution.py:67
  (27 shorter events, 5.0 us)
Async XLA Ops:
  6.5 137.5 %reduce-scatter.3.cloned.1.call-start = ((), (), s32[]{:S(2)}) async-start(), calls=%async_computation.2 | async-start | bytes 17825792 | tf_op jit(solution)/shard_map/reduce_scatter | solution.py:39
  30.3 251.7 %all-gather.4.cloned.1.call-start = ((), (), s32[]{:S(2)}) async-start(), calls=%async_computation.3 | async-start | bytes 8912896 | tf_op jit(solution)/shard_map/all_gather | solution.py:48
  213.7 110.7 %reduce-scatter.5.cloned.1.call-start = ((), (), s32[]{:S(2)}) async-start(), calls=%async_computation.4 | async-start | bytes 4718592 | tf_op jit(solution)/shard_map/reduce_scatter | solution.py:50
  289.8 95.5 %all-gather.6.cloned.1.call-start = ((), (), s32[]{:S(2)}) async-start(), calls=%async_computation.5 | async-start | bytes 4456448 | tf_op jit(solution)/shard_map/all_gather | solution.py:60
  324.4 53.9 %copy-start.1 = (f32[512,256]{1,0:T(8,128)S(1)}, f32[512,256]{1,0:T(8,128)}, u32[]{:S(2)}) copy-start(f32[512,256]{1,0:T(8,128)} %reduce-scatter.5.cloned.1.call-done) | copy-start | bytes 1572868
  326.3 93.4 %all-gather.8.cloned.1.call-start = ((), (), s32[]{:S(2)}) async-start(), calls=%async_computation.6 | async-start | bytes 2359296 | tf_op jit(solution)/shard_map/all_gather | solution.py:68
  326.3 4.9 %collective-permute-start = (bf16[256,512]{0,1:T(8,128)(2,1)}, bf16[256,512]{0,1:T(8,128)(2,1)S(1)}, u32[]{:S(2)}, u32[]{:S(2)}) collective-permute-start(bf16[256,512]{0,1:T(8,128)(2,1)} %convert_bitcast_fusion), channel_id=1, source_target_pairs={{0,1},{1,2},{2,3},{3,4},{4,5},{5,6},{6,7},{7,0},{8,9},{9,10},{10,1... | collective-permute-start | bytes 786440 | tf_op jit(solution)/shard_map/ppermute | solution.py:28
  331.2 7.0 %collective-permute-start.1 = (bf16[256,512]{0,1:T(8,128)(2,1)S(1)}, bf16[256,512]{0,1:T(8,128)(2,1)S(1)}, u32[]{:S(2)}, u32[]{:S(2)}) collective-permute-start(bf16[256,512]{0,1:T(8,128)(2,1)S(1)} %collective-permute-done), channel_id=1, source_target_pairs={{0,1},{1,2},{2,3},{3,4},{4,5},{5,6},{6,7},{7,0},{8,9},{9,10},{10,1... | collective-permute-start | bytes 786440 | tf_op jit(solution)/shard_map/ppermute | solution.py:28
  338.2 7.0 %collective-permute-start.2 = (bf16[256,512]{0,1:T(8,128)(2,1)S(1)}, bf16[256,512]{0,1:T(8,128)(2,1)S(1)}, u32[]{:S(2)}, u32[]{:S(2)}) collective-permute-start(bf16[256,512]{0,1:T(8,128)(2,1)S(1)} %collective-permute-done.1), channel_id=1, source_target_pairs={{0,1},{1,2},{2,3},{3,4},{4,5},{5,6},{6,7},{7,0},{8,9},{9,10},{10,1... | collective-permute-start | bytes 786440 | tf_op jit(solution)/shard_map/ppermute | solution.py:28
  345.2 7.0 %collective-permute-start.3 = (bf16[256,512]{0,1:T(8,128)(2,1)S(1)}, bf16[256,512]{0,1:T(8,128)(2,1)S(1)}, u32[]{:S(2)}, u32[]{:S(2)}) collective-permute-start(bf16[256,512]{0,1:T(8,128)(2,1)S(1)} %collective-permute-done.2), channel_id=1, source_target_pairs={{0,1},{1,2},{2,3},{3,4},{4,5},{5,6},{6,7},{7,0},{8,9},{9,10},{10,1... | collective-permute-start | bytes 786440 | tf_op jit(solution)/shard_map/ppermute | solution.py:28
  352.2 7.0 %collective-permute-start.4 = (bf16[256,512]{0,1:T(8,128)(2,1)S(1)}, bf16[256,512]{0,1:T(8,128)(2,1)S(1)}, u32[]{:S(2)}, u32[]{:S(2)}) collective-permute-start(bf16[256,512]{0,1:T(8,128)(2,1)S(1)} %collective-permute-done.3), channel_id=1, source_target_pairs={{0,1},{1,2},{2,3},{3,4},{4,5},{5,6},{6,7},{7,0},{8,9},{9,10},{10,1... | collective-permute-start | bytes 786440 | tf_op jit(solution)/shard_map/ppermute | solution.py:28
  359.3 7.0 %collective-permute-start.5 = (bf16[256,512]{0,1:T(8,128)(2,1)S(1)}, bf16[256,512]{0,1:T(8,128)(2,1)S(1)}, u32[]{:S(2)}, u32[]{:S(2)}) collective-permute-start(bf16[256,512]{0,1:T(8,128)(2,1)S(1)} %collective-permute-done.4), channel_id=1, source_target_pairs={{0,1},{1,2},{2,3},{3,4},{4,5},{5,6},{6,7},{7,0},{8,9},{9,10},{10,1... | collective-permute-start | bytes 786440 | tf_op jit(solution)/shard_map/ppermute | solution.py:28
  366.3 7.0 %collective-permute-start.6 = (bf16[256,512]{0,1:T(8,128)(2,1)S(1)}, bf16[256,512]{0,1:T(8,128)(2,1)S(1)}, u32[]{:S(2)}, u32[]{:S(2)}) collective-permute-start(bf16[256,512]{0,1:T(8,128)(2,1)S(1)} %collective-permute-done.5), channel_id=1, source_target_pairs={{0,1},{1,2},{2,3},{3,4},{4,5},{5,6},{6,7},{7,0},{8,9},{9,10},{10,1... | collective-permute-start | bytes 786440 | tf_op jit(solution)/shard_map/ppermute | solution.py:28
  374.0 11.3 %copy-start.2 = (bf16[256,512]{0,1:T(8,128)(2,1)S(1)}, bf16[256,512]{0,1:T(8,128)(2,1)}, u32[]{:S(2)}) copy-start(bf16[256,512]{0,1:T(8,128)(2,1)} %convert_bitcast_fusion) | copy-start | bytes 786436
  384.9 34.8 %copy-start = (bf16[256,1024]{1,0:T(8,128)(2,1)S(1)}, bf16[256,1024]{1,0:T(8,128)(2,1)}, u32[]{:S(2)}) copy-start(bf16[256,1024]{1,0:T(8,128)(2,1)} %multiply_convert_fusion) | copy-start | bytes 1572868
Sparse Core Ops, SparseCore 0:
  30.4 113.5 reduce-scatter.2
  213.8 68.1 all-gather.3
  289.9 34.4 reduce-scatter.4
  326.4 58.8 all-gather.5
  390.2 29.3 all-gather.7
